TPU v7x, 32 devices: a whole 2x2x4 slice. The times are simulated.
32 devices in a mesh: tok: 16 (over z, y, x), hid: 2 (over core).
Axes of the slice: x: 2, y: 2, z: 4, core: 2. Of those that a mesh axis runs over, the one named last changes fastest.
Arguments:
- acts: bfloat16 [4096, 28672], P('tok', 'hid'), may hold values from -6 to 6
- out_grads: bfloat16 [4096, 8192], P('tok', 'hid'), may hold values from -0.119628906 to 0.119628906
- proj_in: bfloat16 [28672, 64], P('hid'), may hold values from -0.03125 to 0.03125
- proj_out: bfloat16 [8192, 64], P('hid'), may hold values from -0.0625 to 0.0625
- example_ids: int32 [4096], P('tok'), may hold values from 0 to 3, never falling along the last dimension, each value on 1 to 2048 neighbouring positions
- queries: float32 [1024, 4096], P(None, 'tok'), may hold values from -0.09375 to 0.09375
- precond: float32 [4096, 4096], P('tok', 'hid'), may hold values from -0.09375 to 0.09375
Outputs:
- scores: float32 [1024, 4], P('tok')
- features: float32 [4, 4096], P(None, 'hid')
Inputs may be any that keep to these rules, and one draw needn't show every extreme that they name: `example_ids`: ids never fall along the tokens; each example holds 1 to 2048 tokens, and one holds exactly 2048.
All inputs are finite; a program needn't handle non-finite values.
Results may differ from a plain program's by a relative error of at most 0.0003.
Values sent between devices are 32-bit elements; how exact they have to be, the bound alone decides.
A program may use at most 64 MiB of HBM per device.

v0:
```python
import functools

import jax
import jax.numpy as jnp
from jax import lax
from jax.experimental import pallas as pl
from jax.experimental.pallas import tpu as pltpu
from jax.sharding import PartitionSpec as P

EX_LEN = 2048
MESH = pl.DeviceIdType.MESH
BF, F32 = jnp.bfloat16, jnp.float32


def nt(a, b):
    return lax.dot_general(a, b, (((1,), (1,)), ((), ())), preferred_element_type=F32)


def split(x):
    hi = x.astype(BF)
    return hi, (x - hi.astype(F32)).astype(BF)


def kernel(
    T, H, A, E, ci, co,
    acts, grads, pin, pout, ids, queries, precond,
    scores_out, feats_out,
    acts_v, grads_v, pin_v, pout_v, ids_v, q_v, p_v,
    q_hi, q_lo, p_hi, p_lo,
    inner_v, outer_v, inner_r, outer_r, r_v, w_v, y_v, rs_r, z_v, own_v, full_v,
    f2_v, im2_v, sc_v, s_v,
    ld_sem, in_sem, hs_sem, hr_sem, as_sem, ar_sem, zs_sem, zr_sem, gs_sem, gr_sem,
    ss_sem, sr_sem,
):
    B = T // A
    t, h = lax.axis_index("tok"), lax.axis_index("hid")
    a, b = lax.rem(t, A), lax.div(t, A)
    width, tokens = inner_v.shape
    slab = width // H
    half = slab // 2
    part = half // A

    loads = {}

    def load(name, src, dst):
        c = pltpu.make_async_copy(src, dst, ld_sem.at[len(loads)])
        c.start()
        loads[name] = c

    load("pout", pout, pout_v)
    go = grads.shape[1] // co
    for c in range(co):
        k = pl.ds(c * go, go)
        load(("g", c), grads.at[:, k], grads_v.at[:, k])
    gi = acts.shape[1] // ci
    for c in range(ci):
        k = pl.ds(c * gi, gi)
        load(("pi", c), pin.at[:, k], pin_v.at[:, k])
        load(("a", c), acts.at[:, k], acts_v.at[:, k])
    load("ids", ids, ids_v)
    load("p", precond, p_v)
    load("q", queries, q_v)

    def peer(d):
        return lax.rem(t + d // H, T), lax.rem(h + d % H, H)

    barrier = pltpu.get_barrier_semaphore()
    everyone = T * H - 1

    def greet(d, _):
        pt = lax.rem(t + lax.div(d, H), T)
        ph = lax.rem(h + lax.rem(d, H), H)
        pl.semaphore_signal(barrier, inc=1, device_id=(pt, ph), device_id_type=MESH)
        return 0

    lax.fori_loop(1, T * H, greet, 0, unroll=T * H <= 32)

    loads["pout"].wait()
    acc = jnp.zeros((width, tokens), F32)
    for c in range(co):
        loads[("g", c)].wait()
        k = pl.ds(c * go, go)
        acc = acc + nt(pout_v[:, k], grads_v[:, k])
    outer_v[...] = acc
    acc = jnp.zeros((width, tokens), F32)
    hid_out, hid_in = [], []
    for c in range(ci):
        if c == ci - 1:
            pl.semaphore_wait(barrier, everyone)
            for d in range(1, H):
                ph = lax.rem(h + d, H)
                cp = pltpu.make_async_remote_copy(
                    outer_v, outer_r.at[d - 1], hs_sem.at[0, d - 1], hr_sem.at[0, d - 1],
                    device_id=(t, ph), device_id_type=MESH)
                cp.start()
                hid_out.append(cp)
        loads[("pi", c)].wait()
        loads[("a", c)].wait()
        k = pl.ds(c * gi, gi)
        acc = acc + nt(pin_v[:, k], acts_v[:, k])
    inner_v[...] = acc
    for d in range(1, H):
        ph = lax.rem(h + d, H)
        cp = pltpu.make_async_remote_copy(
            inner_v.at[pl.ds(pl.multiple_of(ph * slab, slab), slab), :], inner_r.at[d - 1],
            hs_sem.at[1, d - 1], hr_sem.at[1, d - 1],
            device_id=(t, ph), device_id_type=MESH)
        cp.start()
        hid_in.append(cp)
    loads["ids"].wait()

    for cp in hid_out:
        cp.wait_recv()
    outer = outer_v[...]
    for d in range(1, H):
        outer = outer + outer_r[d - 1]
    o_hi, o_lo = split(jnp.concatenate([outer, outer], axis=0))
    for cp in hid_in:
        cp.wait_recv()
    inner = inner_v[pl.ds(pl.multiple_of(h * slab, slab), slab), :]
    for d in range(1, H):
        inner = inner + inner_r[d - 1]
    for e in range(E):
        w_v[pl.ds(e * slab, slab), :] = inner * (ids_v[...] == e).astype(F32)
    w_hi, w_lo = split(w_v[...])
    r_v[...] = nt(w_hi, o_hi) + nt(w_hi, o_lo) + nt(w_lo, o_hi)
    left = lax.broadcasted_iota(jnp.int32, (E, 2 * width), 1) < width
    for n in range(half):
        y_v[n] = jnp.where(
            left, r_v[pl.ds(2 * n, E, stride=slab), :], r_v[pl.ds(2 * n + 1, E, stride=slab), :])

    def band(i):
        return pl.ds(i * part, part)

    send = []
    for d in range(1, A):
        pa = lax.rem(a + d, A)
        cp = pltpu.make_async_remote_copy(
            y_v.at[band(pa)], rs_r.at[d - 1], as_sem, ar_sem,
            device_id=(b * A + pa, h), device_id_type=MESH)
        cp.start()
        send.append(cp)
    loads["p"].wait()
    p_hi[...] = p_v[...].astype(BF)
    p_lo[...] = (p_v[...] - p_hi[...].astype(F32)).astype(BF)
    loads["q"].wait()
    q_hi[...] = q_v[...].astype(BF)
    q_lo[...] = (q_v[...] - q_hi[...].astype(F32)).astype(BF)
    mine = y_v[band(a)]
    every = pltpu.make_async_copy(rs_r, rs_r, ar_sem)
    every.wait()
    for d in range(1, A):
        mine = mine + rs_r[d - 1]
    if B > 1:
        own_v[...] = mine
    zsend = []
    for d in range(1, B):
        pb = lax.rem(b + d, B)
        cp = pltpu.make_async_remote_copy(
            own_v, z_v.at[b], zs_sem.at[d - 1], zr_sem.at[b],
            device_id=(pb * A + a, h), device_id_type=MESH)
        cp.start()
        zsend.append(cp)
    if B > 1:
        z_v[b] = mine
    for d in range(1, B):
        pb = lax.rem(b + d, B)
        pltpu.make_async_remote_copy(
            own_v, z_v.at[pb], zs_sem.at[d - 1], zr_sem.at[pb],
            device_id=(pb * A + a, h), device_id_type=MESH).wait_recv()
    total = z_v[0] if B > 1 else mine
    for i in range(1, B):
        total = total + z_v[i]
    full_v[band(a)] = total
    G = min(4, A)
    ag, ai = lax.div(a, G), lax.rem(a, G)

    def gather(dg, di):
        pg = lax.rem(ag + dg, A // G)
        pa = pg * G + lax.rem(ai + di, G)
        return pltpu.make_async_remote_copy(
            full_v.at[band(a)], full_v.at[band(a)], gs_sem, gr_sem.at[ag],
            device_id=(b * A + pa, h), device_id_type=MESH)

    far = sorted(range(A // G), key=lambda g: -min(g, A // G - g))
    for dg in far[::-1]:
        for di in range(G):
            if dg or di:
                gather(dg, di).start()
    lanes = 2 * width
    gp = G * part
    im = jnp.zeros((2 * E, p_hi.shape[0]), F32)
    for dg in far[::-1]:
        pg = lax.rem(ag + dg, A // G)
        n = gp if dg else gp - part
        if n:
            got = full_v.at[pl.ds(0, n)]
            pltpu.make_async_copy(got, got, gr_sem.at[pg]).wait()
        fs = [full_v[pg * gp + i] for i in range(gp)]
        f = jnp.concatenate(fs, axis=1)
        k = pl.ds(pl.multiple_of(pg * (gp * lanes), gp * lanes), gp * lanes)
        f2_v[dg, pl.ds(0, E), :] = f
        f2_v[dg, pl.ds(E, E), :] = f - f.astype(BF).astype(F32)
        fb = f2_v[dg].astype(BF)
        im = im + nt(fb, p_hi[:, k]) + nt(fb, p_lo[:, k])
    im = im[:E] + im[E:]
    im2_v[pl.ds(0, E), :] = im
    im2_v[pl.ds(E, E), :] = im - im.astype(BF).astype(F32)
    ib = im2_v[...].astype(BF)
    sc = nt(ib, q_hi[...]) + nt(ib, q_lo[...])
    sc = sc[:E] + sc[E:]
    tiles = sc.shape[1] // 128
    for n in range(tiles):
        sc_v[n] = sc[:, n * 128:(n + 1) * 128]
    per = T // tiles
    me = t * H + h

    def ssend(d):
        pt = lax.rem(t + lax.rem(d, T), T)
        ph = lax.rem(h + lax.div(d, T), H)
        return pltpu.make_async_remote_copy(
            sc_v.at[lax.div(pt, per)], s_v.at[me], ss_sem, sr_sem,
            device_id=(pt, ph), device_id_type=MESH)

    def loop(fn):
        lax.fori_loop(1, T * H, lambda d, c: (fn(d), c)[1], 0, unroll=T * H <= 32)

    loop(lambda d: ssend(d).start())
    s_v[me] = sc_v[lax.div(t, per)]
    for cp in hid_out + hid_in + zsend:
        cp.wait_send()
    for n in range(half):
        feats_out[:, pl.ds(n * lanes, lanes)] = full_v[n]
    got = s_v.at[pl.ds(0, T * H - 1)]
    pltpu.make_async_copy(got, got, sr_sem).wait()
    if T * H <= 32:
        parts = [s_v[i] for i in range(T * H)]
        while len(parts) > 1:
            parts = [parts[i] + parts[i + 1] for i in range(0, len(parts), 2)]
        tot = parts[0]
    else:
        tot = lax.fori_loop(0, T * H, lambda i, c: c + s_v[i], jnp.zeros(s_v.shape[1:], F32))
    span = 128 // per
    place = lax.rem(t, per)
    res = tot[:, :span]
    for i in range(1, per):
        res = jnp.where(place == i, tot[:, i * span:(i + 1) * span], res)
    scores_out[...] = res
    pltpu.make_async_copy(got, got, ss_sem).wait()
    pltpu.make_async_copy(rs_r, rs_r, as_sem).wait()
    got = full_v.at[pl.ds(0, half - part)]
    pltpu.make_async_copy(got, got, gs_sem).wait()


def finish(scores, feats, scores_out, feats_out):
    scores_out[...] = scores[...]
    feats_out[...] = feats[...]


def on_device(T, H, acts, out_grads, proj_in, proj_out, example_ids, queries, precond):
    tokens = acts.shape[0]
    E = 2 * tokens * T // EX_LEN
    width = proj_in.shape[1]
    slab = width // H
    half = slab // 2
    A = min(T, half)
    B = T // A
    part = half // A
    lanes = 2 * width
    cols = slab * width
    Q, M = queries.shape
    ci, co = 7, 2
    D = pltpu.SemaphoreType.DMA
    V = pltpu.VMEM
    hbm = pl.BlockSpec(memory_space=pl.ANY)
    scores, feats = pl.pallas_call(
        functools.partial(kernel, T, H, A, E, ci, co),
        out_shape=(
            jax.ShapeDtypeStruct((E, Q // T), F32),
            jax.ShapeDtypeStruct((E, cols), F32),
        ),
        in_specs=[hbm] * 7,
        out_specs=(pl.BlockSpec(memory_space=pltpu.VMEM),) * 2,
        scratch_shapes=[
            V(acts.shape, BF), V(out_grads.shape, BF),
            V(proj_in.shape[::-1], BF), V(proj_out.shape[::-1], BF),
            V((1, tokens), jnp.int32), V((Q, M), F32), V(precond.shape, F32),
            V((Q, M), BF), V((Q, M), BF), V(precond.shape, BF), V(precond.shape, BF),
            V((width, tokens), F32), V((width, tokens), F32),
            V((H - 1, slab, tokens), F32), V((H - 1, width, tokens), F32),
            V((E * slab, lanes), F32), V((E * slab, tokens), F32),
            V((half, E, lanes), F32), V((A - 1, part, E, lanes), F32),
            V((B, part, E, lanes), F32), V((part, E, lanes), F32),
            V((half, E, lanes), F32),
            V((A // min(4, A), 2 * E, min(4, A) * part * lanes), F32), V((2 * E, M), F32),
            V((Q // 128, E, 128), F32), V((T * H, E, 128), F32),
            D((5 + co + 2 * ci,)), D, D((2, H - 1)), D((2, H - 1)),
            D, D, D((max(B - 1, 1),)), D((B,)), D, D((A // min(4, A),)),
            D, D,
        ],
        compiler_params=pltpu.CompilerParams(
            collective_id=0, has_side_effects=True, vmem_limit_bytes=60000 * 1024
        ),
    )(acts, out_grads, proj_in.T, proj_out.T, example_ids.reshape(1, tokens), queries, precond)
    scores, feats = pl.pallas_call(
        finish,
        out_shape=(
            jax.ShapeDtypeStruct(scores.shape, F32),
            jax.ShapeDtypeStruct(feats.shape, F32),
        ),
    )(scores, feats)
    return scores.T, feats


def solution(mesh):
    T, H = mesh.shape["tok"], mesh.shape["hid"]
    in_specs = (
        P("tok", "hid"),
        P("tok", "hid"),
        P("hid", None),
        P("hid", None),
        P("tok"),
        P(None, "tok"),
        P("tok", "hid"),
    )
    out_specs = (P("tok", None), P(None, "hid"))
    return jax.shard_map(
        functools.partial(on_device, T, H), mesh=mesh, in_specs=in_specs, out_specs=out_specs,
        check_vma=False,
    )
```

profile of v0, /device:TPU:0, one launch (start us, length us, event | category | flops | bytes accessed | tf_op | source)
XLA Modules:
  0.0 29.2 jit_solution(9150670319631610817)
XLA Ops:
  0.6 27.2 %shard_map.86 = (f32[4,64]{1,0:T(4,128)}, f32[4,2048]{1,0:T(4,128)}) custom-call(bf16[256,14336]{1,0:T(8,128)(2,1)} %acts.1, bf16[256,4096]{1,0:T(8,128)(2,1)} %grads.1, bf16[64,14336]{1,0:T(8,128)(2,1)} %bitcast.4, bf16[64,4096]{1,0:T(8,128)(2,1)} %bitcast.5, s32[1,256]{1,0:T(1,128)} %bitcast.6, f32[1024,256]{1,0:T(8,128)} %queries.1, f32[256,2048]{1,0:T(8,128)} %precond.1), custom_call_target="tpu_custom_call" | custom-call | tf_op jit(solution)/shard_map/pallas_call | solution.py:276
  27.8 1.4 %shard_map.87 = (f32[4,64]{1,0:T(4,128)}, f32[4,2048]{1,0:T(4,128)}) custom-call(f32[4,64]{1,0:T(4,128)} %get-tuple-element.6.scores, f32[4,2048]{1,0:T(4,128)} %get-tuple-element.7.feats), custom_call_target="tpu_custom_call" | custom-call | tf_op jit(solution)/shard_map/pallas_call | solution.py:305
where the time goes:
time: 29.4 us; the launch traced here: 29.2 us
  Pallas kernels  28.5 us (97%)
  between operations  0.64 us (2%)
    pallas_call x1, Pallas kernels, on_device(): pl.pallas_call(functools.partial(kernel, T, H, A, E, ci, co), out_shape=(...  27.2 us
    pallas_call x1, Pallas kernels, on_device(): pl.pallas_call(finish, out_shape=(jax.ShapeDtypeStruct(scores.shape, F32)...  1.38 us

commit v1 on v0

--- a/solution.py
+++ b/solution.py
@@ -8,17 +8,22 @@
 from jax.sharding import PartitionSpec as P
 
 EX_LEN = 2048
+TILE = 256
 MESH = pl.DeviceIdType.MESH
 BF, F32 = jnp.bfloat16, jnp.float32
-
-
-def nt(a, b):
-    return lax.dot_general(a, b, (((1,), (1,)), ((), ())), preferred_element_type=F32)
 
 
 def split(x):
     hi = x.astype(BF)
     return hi, (x - hi.astype(F32)).astype(BF)
+
+
+def fill(pair, src, at):
+    for ref in pair:
+        if ref.shape != src.shape:
+            ref[...] = jnp.zeros(ref.shape, BF)
+    for ref, half in zip(pair, split(src[...])):
+        ref[at] = half
 
 
 def kernel(
@@ -75,30 +80,40 @@
 
     lax.fori_loop(1, T * H, greet, 0, unroll=T * H <= 32)
 
-    loads["pout"].wait()
-    acc = jnp.zeros((width, tokens), F32)
-    for c in range(co):
-        loads[("g", c)].wait()
-        k = pl.ds(c * go, go)
-        acc = acc + nt(pout_v[:, k], grads_v[:, k])
-    outer_v[...] = acc
-    acc = jnp.zeros((width, tokens), F32)
     hid_out, hid_in = [], []
-    for c in range(ci):
-        if c == ci - 1:
-            pl.semaphore_wait(barrier, everyone)
-            for d in range(1, H):
-                ph = lax.rem(h + d, H)
-                cp = pltpu.make_async_remote_copy(
-                    outer_v, outer_r.at[d - 1], hs_sem.at[0, d - 1], hr_sem.at[0, d - 1],
-                    device_id=(t, ph), device_id_type=MESH)
-                cp.start()
-                hid_out.append(cp)
-        loads[("pi", c)].wait()
-        loads[("a", c)].wait()
-        k = pl.ds(c * gi, gi)
-        acc = acc + nt(pin_v[:, k], acts_v[:, k])
-    inner_v[...] = acc
+    for d in range(1, H):
+        hid_out.append(pltpu.make_async_remote_copy(
+            outer_v, outer_r.at[d - 1], hs_sem.at[0, d - 1], hr_sem.at[0, d - 1],
+            device_id=(t, lax.rem(h + d, H)), device_id_type=MESH))
+
+    def project(*accs):
+        step = 0
+
+        def tiles(x, y, start, size, pair):
+            nonlocal step
+            for j in range(0, size, TILE):
+                k = pl.ds(start + j, TILE)
+                unit, slot = step % 2, step // 2 % 2
+                pltpu.matmul_push_rhs(y[:, k], slot, unit, transpose=True)
+                pltpu.matmul_acc_lhs(pair[unit], x[:, k], slot)
+                step += 1
+
+        loads["pout"].wait()
+        for c in range(co):
+            loads[("g", c)].wait()
+            tiles(pout_v, grads_v, c * go, go, accs[:2])
+        outer_v[...] = pltpu.matmul_pop(accs[0]) + pltpu.matmul_pop(accs[1])
+        for c in range(ci):
+            if c == ci - 1:
+                pl.semaphore_wait(barrier, everyone)
+                for cp in hid_out:
+                    cp.start()
+            loads[("pi", c)].wait()
+            loads[("a", c)].wait()
+            tiles(pin_v, acts_v, c * gi, gi, accs[2:])
+        inner_v[...] = pltpu.matmul_pop(accs[2]) + pltpu.matmul_pop(accs[3])
+
+    pl.run_scoped(project, *[pltpu.ACC(u)((width, tokens), F32) for u in (0, 1, 0, 1)])
     for d in range(1, H):
         ph = lax.rem(h + d, H)
         cp = pltpu.make_async_remote_copy(
@@ -122,8 +137,18 @@
         inner = inner + inner_r[d - 1]
     for e in range(E):
         w_v[pl.ds(e * slab, slab), :] = inner * (ids_v[...] == e).astype(F32)
-    w_hi, w_lo = split(w_v[...])
-    r_v[...] = nt(w_hi, o_hi) + nt(w_hi, o_lo) + nt(w_lo, o_hi)
+
+    def combine(*accs):
+        o = jnp.concatenate([o_hi, o_lo], axis=0)
+        for unit, w in enumerate(split(w_v[...])):
+            for j in range(0, tokens, TILE):
+                slot = j // TILE % 2
+                pltpu.matmul_push_rhs(o[:, j:j + TILE], slot, unit, transpose=True)
+                pltpu.matmul_acc_lhs(accs[unit], w[:, j:j + TILE], slot)
+        r = pltpu.matmul_pop(accs[0]) + pltpu.matmul_pop(accs[1])
+        r_v[...] = r[:, :2 * width] + r[:, 2 * width:]
+
+    pl.run_scoped(combine, *[pltpu.ACC(u)((E * slab, TILE), F32) for u in (0, 1)])
     left = lax.broadcasted_iota(jnp.int32, (E, 2 * width), 1) < width
     for n in range(half):
         y_v[n] = jnp.where(
@@ -141,11 +166,12 @@
         cp.start()
         send.append(cp)
     loads["p"].wait()
-    p_hi[...] = p_v[...].astype(BF)
-    p_lo[...] = (p_v[...] - p_hi[...].astype(F32)).astype(BF)
+    M = p_v.shape[0]
+    fill((p_hi, p_lo), p_v, (pl.ds(0, M), slice(None)))
     loads["q"].wait()
-    q_hi[...] = q_v[...].astype(BF)
-    q_lo[...] = (q_v[...] - q_hi[...].astype(F32)).astype(BF)
+    fill((q_hi, q_lo), q_v, (slice(None), pl.ds(0, M)))
+    f2_v[...] = jnp.zeros(f2_v.shape, F32)
+    im2_v[...] = jnp.zeros(im2_v.shape, F32)
     mine = y_v[band(a)]
     every = pltpu.make_async_copy(rs_r, rs_r, ar_sem)
     every.wait()
@@ -189,29 +215,68 @@
                 gather(dg, di).start()
     lanes = 2 * width
     gp = G * part
-    im = jnp.zeros((2 * E, p_hi.shape[0]), F32)
-    for dg in far[::-1]:
-        pg = lax.rem(ag + dg, A // G)
-        n = gp if dg else gp - part
-        if n:
-            got = full_v.at[pl.ds(0, n)]
-            pltpu.make_async_copy(got, got, gr_sem.at[pg]).wait()
-        fs = [full_v[pg * gp + i] for i in range(gp)]
-        f = jnp.concatenate(fs, axis=1)
-        k = pl.ds(pl.multiple_of(pg * (gp * lanes), gp * lanes), gp * lanes)
-        f2_v[dg, pl.ds(0, E), :] = f
-        f2_v[dg, pl.ds(E, E), :] = f - f.astype(BF).astype(F32)
-        fb = f2_v[dg].astype(BF)
-        im = im + nt(fb, p_hi[:, k]) + nt(fb, p_lo[:, k])
-    im = im[:E] + im[E:]
-    im2_v[pl.ds(0, E), :] = im
-    im2_v[pl.ds(E, E), :] = im - im.astype(BF).astype(F32)
-    ib = im2_v[...].astype(BF)
-    sc = nt(ib, q_hi[...]) + nt(ib, q_lo[...])
-    sc = sc[:E] + sc[E:]
-    tiles = sc.shape[1] // 128
-    for n in range(tiles):
-        sc_v[n] = sc[:, n * 128:(n + 1) * 128]
+    groups = far[::-1]
+    cuts = gp * lanes // TILE
+    Q = q_hi.shape[0]
+    tiles = Q // 128
+
+    def score(im_hi, im_lo, *outs):
+        rows = []
+        for dg in groups:
+            pg = lax.rem(ag + dg, A // G)
+            for j in range(cuts):
+                rows.append(pl.ds(pl.multiple_of(pg * (gp * lanes) + j * TILE, TILE), TILE))
+
+        def push(n):
+            for unit, p in enumerate((p_hi, p_lo)):
+                pltpu.matmul_push_rhs(p[:, rows[n]], n % 2, unit, transpose=True)
+
+        def push_q(n):
+            for slot, q in enumerate((q_hi, q_lo)):
+                pltpu.matmul_push_rhs(q[pl.ds(n * TILE, TILE), :], slot, n % 2, transpose=True)
+
+        for n in range(min(2, len(rows))):
+            push(n)
+        step = 0
+        for dg in groups:
+            pg = lax.rem(ag + dg, A // G)
+            n = gp if dg else gp - part
+            if n:
+                got = full_v.at[pl.ds(0, n)]
+                pltpu.make_async_copy(got, got, gr_sem.at[pg]).wait()
+            f = jnp.concatenate([full_v[pg * gp + i] for i in range(gp)], axis=1)
+            f2_v[dg, pl.ds(0, E), :] = f
+            f2_v[dg, pl.ds(E, E), :] = f - f.astype(BF).astype(F32)
+            fb = f2_v[dg].astype(BF)
+            for j in range(cuts):
+                for acc in (im_hi, im_lo):
+                    pltpu.matmul_acc_lhs(acc, fb[:, j * TILE:(j + 1) * TILE], step % 2)
+                if step + 2 < len(rows):
+                    push(step + 2)
+                step += 1
+        for n in range(min(2, Q // TILE)):
+            push_q(n)
+        im = pltpu.matmul_pop(im_hi) + pltpu.matmul_pop(im_lo)
+        im = im[:E, :M] + im[E:2 * E, :M]
+        im2_v[pl.ds(0, E), pl.ds(0, M)] = im
+        im2_v[pl.ds(E, E), pl.ds(0, M)] = im - im.astype(BF).astype(F32)
+        ib = im2_v[...].astype(BF)
+        for n in range(Q // TILE):
+            for slot in range(2):
+                pltpu.matmul_acc_lhs(outs[n], ib, slot)
+            if n + 2 < Q // TILE:
+                push_q(n + 2)
+        for n in range(Q // TILE):
+            sc = pltpu.matmul_pop(outs[n])
+            sc = sc[:E] + sc[E:2 * E]
+            for i in range(TILE // 128):
+                sc_v[n * (TILE // 128) + i] = sc[:, i * 128:(i + 1) * 128]
+
+    tall = im2_v.shape[0]
+    pl.run_scoped(
+        score,
+        *[pltpu.ACC(u)((tall, TILE), F32) for u in (0, 1)],
+        *[pltpu.ACC(n % 2)((tall, TILE), F32) for n in range(Q // TILE)])
     per = T // tiles
     me = t * H + h
 
@@ -269,7 +334,8 @@
     lanes = 2 * width
     cols = slab * width
     Q, M = queries.shape
-    ci, co = 7, 2
+    ci, co = 14, 4
+    tall = -(-2 * E // 16) * 16
     D = pltpu.SemaphoreType.DMA
     V = pltpu.VMEM
     hbm = pl.BlockSpec(memory_space=pl.ANY)
@@ -285,14 +351,15 @@
             V(acts.shape, BF), V(out_grads.shape, BF),
             V(proj_in.shape[::-1], BF), V(proj_out.shape[::-1], BF),
             V((1, tokens), jnp.int32), V((Q, M), F32), V(precond.shape, F32),
-            V((Q, M), BF), V((Q, M), BF), V(precond.shape, BF), V(precond.shape, BF),
+            V((Q, TILE), BF), V((Q, TILE), BF),
+            V((TILE, precond.shape[1]), BF), V((TILE, precond.shape[1]), BF),
             V((width, tokens), F32), V((width, tokens), F32),
             V((H - 1, slab, tokens), F32), V((H - 1, width, tokens), F32),
             V((E * slab, lanes), F32), V((E * slab, tokens), F32),
             V((half, E, lanes), F32), V((A - 1, part, E, lanes), F32),
             V((B, part, E, lanes), F32), V((part, E, lanes), F32),
             V((half, E, lanes), F32),
-            V((A // min(4, A), 2 * E, min(4, A) * part * lanes), F32), V((2 * E, M), F32),
+            V((A // min(4, A), tall, min(4, A) * part * lanes), F32), V((tall, TILE), F32),
             V((Q // 128, E, 128), F32), V((T * H, E, 128), F32),
             D((5 + co + 2 * ci,)), D, D((2, H - 1)), D((2, H - 1)),
             D, D, D((max(B - 1, 1),)), D((B,)), D, D((A // min(4, A),)),

time: 29.4 us -> 26.8 us (0.912)
  Pallas kernels: 28.5 us -> 26 us
    pallas_call x1, Pallas kernels: 27.2 us -> 24.6 us  [on_device(): pl.pallas_call(functools.partial(kernel, T, H, A, E, ci, co), out_shape=(...]
where the time goes in v1:
time: 26.8 us; the launch traced here: 26.6 us
  Pallas kernels  26 us (97%)
  between operations  0.64 us (2%)
    pallas_call x1, Pallas kernels, on_device(): pl.pallas_call(functools.partial(kernel, T, H, A, E, ci, co), out_shape=(...  24.6 us
    pallas_call x1, Pallas kernels, on_device(): pl.pallas_call(finish, out_shape=(jax.ShapeDtypeStruct(scores.shape, F32)...  1.38 us

profile of v1, /device:TPU:0, one launch (start us, length us, event | category | flops | bytes accessed | tf_op | source)
XLA Modules:
  0.0 26.6 jit_solution(17953503806799436207)
XLA Ops:
  0.6 24.6 %shard_map.86 = (f32[4,64]{1,0:T(4,128)}, f32[4,2048]{1,0:T(4,128)}) custom-call(bf16[256,14336]{1,0:T(8,128)(2,1)} %acts.1, bf16[256,4096]{1,0:T(8,128)(2,1)} %grads.1, bf16[64,14336]{1,0:T(8,128)(2,1)} %bitcast.4, bf16[64,4096]{1,0:T(8,128)(2,1)} %bitcast.5, s32[1,256]{1,0:T(1,128)} %bitcast.6, f32[1024,256]{1,0:T(8,128)} %queries.1, f32[256,2048]{1,0:T(8,128)} %precond.1), custom_call_target="tpu_custom_call" | custom-call | tf_op jit(solution)/shard_map/pallas_call | solution.py:342
  25.2 1.4 %shard_map.87 = (f32[4,64]{1,0:T(4,128)}, f32[4,2048]{1,0:T(4,128)}) custom-call(f32[4,64]{1,0:T(4,128)} %get-tuple-element.6.scores, f32[4,2048]{1,0:T(4,128)} %get-tuple-element.7.feats), custom_call_target="tpu_custom_call" | custom-call | tf_op jit(solution)/shard_map/pallas_call | solution.py:372

commit v2 on v1

--- a/solution.py
+++ b/solution.py
@@ -338,7 +338,7 @@
     tall = -(-2 * E // 16) * 16
     D = pltpu.SemaphoreType.DMA
     V = pltpu.VMEM
-    hbm = pl.BlockSpec(memory_space=pl.ANY)
+    hbm = pl.BlockSpec(memory_space=pltpu.HBM)
     scores, feats = pl.pallas_call(
         functools.partial(kernel, T, H, A, E, ci, co),
         out_shape=(
@@ -366,15 +366,17 @@
             D, D,
         ],
         compiler_params=pltpu.CompilerParams(
-            collective_id=0, has_side_effects=True, vmem_limit_bytes=60000 * 1024
+            collective_id=0, has_side_effects=True, vmem_limit_bytes=32000 * 1024
         ),
-    )(acts, out_grads, proj_in.T, proj_out.T, example_ids.reshape(1, tokens), queries, precond)
+    )(*[pltpu.with_memory_space_constraint(x, pltpu.HBM) for x in (
+        acts, out_grads, proj_in.T, proj_out.T, example_ids.reshape(1, tokens), queries, precond)])
     scores, feats = pl.pallas_call(
         finish,
         out_shape=(
             jax.ShapeDtypeStruct(scores.shape, F32),
             jax.ShapeDtypeStruct(feats.shape, F32),
         ),
+        compiler_params=pltpu.CompilerParams(vmem_limit_bytes=1024 * 1024),
     )(scores, feats)
     return scores.T, feats
 

time: 26.8 us -> 25.4 us (0.948)
  Pallas kernels: 26 us -> 24.6 us
    pallas_call x1, Pallas kernels: 1.38 us -> 0.62 us  [on_device(): pl.pallas_call(finish, out_shape=(jax.ShapeDtypeStruct(scores.shape, F32)...]
    pallas_call x1, Pallas kernels: 24.6 us -> 24 us  [on_device(): pl.pallas_call(functools.partial(kernel, T, H, A, E, ci, co), out_shape=(...]
where the time goes in v2:
time: 25.4 us; the launch traced here: 25.3 us
  Pallas kernels  24.6 us (97%)
  between operations  0.64 us (3%)
    pallas_call x1, Pallas kernels, on_device(): pl.pallas_call(functools.partial(kernel, T, H, A, E, ci, co), out_shape=(...  24 us
    pallas_call x1, Pallas kernels, on_device(): pl.pallas_call(finish, out_shape=(jax.ShapeDtypeStruct(scores.shape, F32)...  0.62 us

profile of v2, /device:TPU:0, one launch (start us, length us, event | category | flops | bytes accessed | tf_op | source)
XLA Modules:
  0.0 25.3 jit_solution(2985225094955487212)
XLA Ops:
  0.6 24.0 %shard_map.86 = (f32[4,64]{1,0:T(4,128)S(1)}, f32[4,2048]{1,0:T(4,128)S(1)}) custom-call(bf16[256,14336]{1,0:T(8,128)(2,1)} %acts.1, bf16[256,4096]{1,0:T(8,128)(2,1)} %grads.1, bf16[64,14336]{1,0:T(8,128)(2,1)} %bitcast.4, bf16[64,4096]{1,0:T(8,128)(2,1)} %bitcast.5, s32[1,256]{1,0:T(1,128)} %bitcast.6, f32[1024,256]{1,0:T(8,128)} %queries.1, ...), custom_call_target="tpu_custom_call" | custom-call | tf_op jit(solution)/shard_map/pallas_call | solution.py:342
  24.6 0.6 %shard_map.87 = (f32[4,64]{1,0:T(4,128)}, f32[4,2048]{1,0:T(4,128)}) custom-call(f32[4,64]{1,0:T(4,128)S(1)} %get-tuple-element.6.scores, f32[4,2048]{1,0:T(4,128)S(1)} %get-tuple-element.7.feats), custom_call_target="tpu_custom_call" | custom-call | tf_op jit(solution)/shard_map/pallas_call | solution.py:373

commit v3 on v2

--- a/solution.py
+++ b/solution.py
@@ -32,9 +32,9 @@
     scores_out, feats_out,
     acts_v, grads_v, pin_v, pout_v, ids_v, q_v, p_v,
     q_hi, q_lo, p_hi, p_lo,
-    inner_v, outer_v, inner_r, outer_r, r_v, w_v, y_v, rs_r, z_v, own_v, full_v,
+    inner_v, outer_v, inner_r, outer_r, r_v, w_v, y_v, rs_r, all_v, full_v,
     f2_v, im2_v, sc_v, s_v,
-    ld_sem, in_sem, hs_sem, hr_sem, as_sem, ar_sem, zs_sem, zr_sem, gs_sem, gr_sem,
+    ld_sem, in_sem, hs_sem, hr_sem, as_sem, ar_sem, gs_sem, gr_sem,
     ss_sem, sr_sem,
 ):
     B = T // A
@@ -177,55 +177,32 @@
     every.wait()
     for d in range(1, A):
         mine = mine + rs_r[d - 1]
-    if B > 1:
-        own_v[...] = mine
-    zsend = []
-    for d in range(1, B):
-        pb = lax.rem(b + d, B)
-        cp = pltpu.make_async_remote_copy(
-            own_v, z_v.at[b], zs_sem.at[d - 1], zr_sem.at[b],
-            device_id=(pb * A + a, h), device_id_type=MESH)
-        cp.start()
-        zsend.append(cp)
-    if B > 1:
-        z_v[b] = mine
-    for d in range(1, B):
-        pb = lax.rem(b + d, B)
-        pltpu.make_async_remote_copy(
-            own_v, z_v.at[pb], zs_sem.at[d - 1], zr_sem.at[pb],
-            device_id=(pb * A + a, h), device_id_type=MESH).wait_recv()
-    total = z_v[0] if B > 1 else mine
+    all_v[b, band(a)] = mine
+
+    def gather(db, da):
+        pb, pa = lax.rem(b + db, B), lax.rem(a + da, A)
+        return pltpu.make_async_remote_copy(
+            all_v.at[b, band(a)], all_v.at[b, band(a)], gs_sem, gr_sem.at[b],
+            device_id=(pb * A + pa, h), device_id_type=MESH)
+
+    for db in sorted(range(B), key=lambda g: -min(g, B - g)):
+        for da in range(A)[::-1]:
+            if db or da:
+                gather(db, da).start()
+    for db in range(B):
+        got = all_v.at[0, pl.ds(0, half if db else half - part)]
+        pltpu.make_async_copy(got, got, gr_sem.at[lax.rem(b + db, B)]).wait()
+    total = all_v[0]
     for i in range(1, B):
-        total = total + z_v[i]
-    full_v[band(a)] = total
-    G = min(4, A)
-    ag, ai = lax.div(a, G), lax.rem(a, G)
-
-    def gather(dg, di):
-        pg = lax.rem(ag + dg, A // G)
-        pa = pg * G + lax.rem(ai + di, G)
-        return pltpu.make_async_remote_copy(
-            full_v.at[band(a)], full_v.at[band(a)], gs_sem, gr_sem.at[ag],
-            device_id=(b * A + pa, h), device_id_type=MESH)
-
-    far = sorted(range(A // G), key=lambda g: -min(g, A // G - g))
-    for dg in far[::-1]:
-        for di in range(G):
-            if dg or di:
-                gather(dg, di).start()
+        total = total + all_v[i]
+    full_v[...] = total
     lanes = 2 * width
-    gp = G * part
-    groups = far[::-1]
-    cuts = gp * lanes // TILE
+    cuts = half * lanes // TILE
     Q = q_hi.shape[0]
     tiles = Q // 128
 
     def score(im_hi, im_lo, *outs):
-        rows = []
-        for dg in groups:
-            pg = lax.rem(ag + dg, A // G)
-            for j in range(cuts):
-                rows.append(pl.ds(pl.multiple_of(pg * (gp * lanes) + j * TILE, TILE), TILE))
+        rows = [pl.ds(j * TILE, TILE) for j in range(cuts)]
 
         def push(n):
             for unit, p in enumerate((p_hi, p_lo)):
@@ -237,23 +214,15 @@
 
         for n in range(min(2, len(rows))):
             push(n)
-        step = 0
-        for dg in groups:
-            pg = lax.rem(ag + dg, A // G)
-            n = gp if dg else gp - part
-            if n:
-                got = full_v.at[pl.ds(0, n)]
-                pltpu.make_async_copy(got, got, gr_sem.at[pg]).wait()
-            f = jnp.concatenate([full_v[pg * gp + i] for i in range(gp)], axis=1)
-            f2_v[dg, pl.ds(0, E), :] = f
-            f2_v[dg, pl.ds(E, E), :] = f - f.astype(BF).astype(F32)
-            fb = f2_v[dg].astype(BF)
-            for j in range(cuts):
-                for acc in (im_hi, im_lo):
-                    pltpu.matmul_acc_lhs(acc, fb[:, j * TILE:(j + 1) * TILE], step % 2)
-                if step + 2 < len(rows):
-                    push(step + 2)
-                step += 1
+        f = jnp.concatenate([full_v[i] for i in range(half)], axis=1)
+        f2_v[pl.ds(0, E), :] = f
+        f2_v[pl.ds(E, E), :] = f - f.astype(BF).astype(F32)
+        fb = f2_v[...].astype(BF)
+        for j in range(cuts):
+            for acc in (im_hi, im_lo):
+                pltpu.matmul_acc_lhs(acc, fb[:, j * TILE:(j + 1) * TILE], j % 2)
+            if j + 2 < cuts:
+                push(j + 2)
         for n in range(min(2, Q // TILE)):
             push_q(n)
         im = pltpu.matmul_pop(im_hi) + pltpu.matmul_pop(im_lo)
@@ -292,7 +261,7 @@
 
     loop(lambda d: ssend(d).start())
     s_v[me] = sc_v[lax.div(t, per)]
-    for cp in hid_out + hid_in + zsend:
+    for cp in hid_out + hid_in:
         cp.wait_send()
     for n in range(half):
         feats_out[:, pl.ds(n * lanes, lanes)] = full_v[n]
@@ -313,8 +282,9 @@
     scores_out[...] = res
     pltpu.make_async_copy(got, got, ss_sem).wait()
     pltpu.make_async_copy(rs_r, rs_r, as_sem).wait()
-    got = full_v.at[pl.ds(0, half - part)]
-    pltpu.make_async_copy(got, got, gs_sem).wait()
+    for n in [half] * (B - 1) + [half - part]:
+        got = all_v.at[0, pl.ds(0, n)]
+        pltpu.make_async_copy(got, got, gs_sem).wait()
 
 
 def finish(scores, feats, scores_out, feats_out):
@@ -328,7 +298,7 @@
     width = proj_in.shape[1]
     slab = width // H
     half = slab // 2
-    A = min(T, half)
+    A = min(T, half, 8)
     B = T // A
     part = half // A
     lanes = 2 * width
@@ -357,12 +327,11 @@
             V((H - 1, slab, tokens), F32), V((H - 1, width, tokens), F32),
             V((E * slab, lanes), F32), V((E * slab, tokens), F32),
             V((half, E, lanes), F32), V((A - 1, part, E, lanes), F32),
-            V((B, part, E, lanes), F32), V((part, E, lanes), F32),
-            V((half, E, lanes), F32),
-            V((A // min(4, A), tall, min(4, A) * part * lanes), F32), V((tall, TILE), F32),
+            V((B, half, E, lanes), F32), V((half, E, lanes), F32),
+            V((tall, half * lanes), F32), V((tall, TILE), F32),
             V((Q // 128, E, 128), F32), V((T * H, E, 128), F32),
             D((5 + co + 2 * ci,)), D, D((2, H - 1)), D((2, H - 1)),
-            D, D, D((max(B - 1, 1),)), D((B,)), D, D((A // min(4, A),)),
+            D, D, D, D((B,)),
             D, D,
         ],
         compiler_params=pltpu.CompilerParams(

time: 25.4 us -> 24 us (0.945)
  Pallas kernels: 24.6 us -> 23.2 us
    pallas_call x1, Pallas kernels: 24 us -> 22.6 us  [on_device(): pl.pallas_call(functools.partial(kernel, T, H, A, E, ci, co), out_shape=(...]
where the time goes in v3:
time: 24 us; the launch traced here: 23.8 us
  Pallas kernels  23.2 us (97%)
  between operations  0.64 us (3%)
    pallas_call x1, Pallas kernels, on_device(): pl.pallas_call(functools.partial(kernel, T, H, A, E, ci, co), out_shape=(...  22.6 us
    pallas_call x1, Pallas kernels, on_device(): pl.pallas_call(finish, out_shape=(jax.ShapeDtypeStruct(scores.shape, F32)...  0.62 us

profile of v3, /device:TPU:0, one launch (start us, length us, event | category | flops | bytes accessed | tf_op | source)
XLA Modules:
  0.0 23.8 jit_solution(15028669198468166374)
XLA Ops:
  0.6 22.6 %shard_map.86 = (f32[4,64]{1,0:T(4,128)S(1)}, f32[4,2048]{1,0:T(4,128)S(1)}) custom-call(bf16[256,14336]{1,0:T(8,128)(2,1)} %acts.1, bf16[256,4096]{1,0:T(8,128)(2,1)} %grads.1, bf16[64,14336]{1,0:T(8,128)(2,1)} %bitcast.4, bf16[64,4096]{1,0:T(8,128)(2,1)} %bitcast.5, s32[1,256]{1,0:T(1,128)} %bitcast.6, f32[1024,256]{1,0:T(8,128)} %queries.1, ...), custom_call_target="tpu_custom_call" | custom-call | tf_op jit(solution)/shard_map/pallas_call | solution.py:312
  23.2 0.6 %shard_map.87 = (f32[4,64]{1,0:T(4,128)}, f32[4,2048]{1,0:T(4,128)}) custom-call(f32[4,64]{1,0:T(4,128)S(1)} %get-tuple-element.6.scores, f32[4,2048]{1,0:T(4,128)S(1)} %get-tuple-element.7.feats), custom_call_target="tpu_custom_call" | custom-call | tf_op jit(solution)/shard_map/pallas_call | solution.py:342

commit v4 on v3

--- a/solution.py
+++ b/solution.py
@@ -178,31 +178,33 @@
     for d in range(1, A):
         mine = mine + rs_r[d - 1]
     all_v[b, band(a)] = mine
+    each = TILE // (2 * width)
+    opt = each // part
 
     def gather(db, da):
         pb, pa = lax.rem(b + db, B), lax.rem(a + da, A)
         return pltpu.make_async_remote_copy(
-            all_v.at[b, band(a)], all_v.at[b, band(a)], gs_sem, gr_sem.at[b],
+            all_v.at[b, band(a)], all_v.at[b, band(a)], gs_sem, gr_sem.at[b, lax.div(a, opt)],
             device_id=(pb * A + pa, h), device_id_type=MESH)
 
     for db in sorted(range(B), key=lambda g: -min(g, B - g)):
         for da in range(A)[::-1]:
             if db or da:
                 gather(db, da).start()
-    for db in range(B):
-        got = all_v.at[0, pl.ds(0, half if db else half - part)]
-        pltpu.make_async_copy(got, got, gr_sem.at[lax.rem(b + db, B)]).wait()
-    total = all_v[0]
-    for i in range(1, B):
-        total = total + all_v[i]
-    full_v[...] = total
     lanes = 2 * width
     cuts = half * lanes // TILE
     Q = q_hi.shape[0]
-    tiles = Q // 128
+    span = Q // T
+    deep = E * span // 128
 
     def score(im_hi, im_lo, *outs):
-        rows = [pl.ds(j * TILE, TILE) for j in range(cuts)]
+        G = min(4, cuts)
+        first = lax.div(a, opt)
+        turn = []
+        for d in range(cuts):
+            far = lax.rem(lax.div(first, G) + d // G, cuts // G)
+            turn.append(far * G + lax.rem(lax.rem(first, G) + d % G, G))
+        rows = [pl.ds(pl.multiple_of(j * TILE, TILE), TILE) for j in turn]
 
         def push(n):
             for unit, p in enumerate((p_hi, p_lo)):
@@ -214,15 +216,25 @@
 
         for n in range(min(2, len(rows))):
             push(n)
-        f = jnp.concatenate([full_v[i] for i in range(half)], axis=1)
-        f2_v[pl.ds(0, E), :] = f
-        f2_v[pl.ds(E, E), :] = f - f.astype(BF).astype(F32)
-        fb = f2_v[...].astype(BF)
-        for j in range(cuts):
+        for d in range(cuts):
+            for db in range(B):
+                n = each if d or db else each - part
+                if n:
+                    got = all_v.at[0, pl.ds(0, n)]
+                    pltpu.make_async_copy(got, got, gr_sem.at[lax.rem(b + db, B), turn[d]]).wait()
+            at = pl.ds(turn[d] * each, each)
+            total = all_v[0, at]
+            for i in range(1, B):
+                total = total + all_v[i, at]
+            full_v[at] = total
+            f = jnp.concatenate([total[i] for i in range(each)], axis=1)
+            f2_v[d, pl.ds(0, E), :] = f
+            f2_v[d, pl.ds(E, E), :] = f - f.astype(BF).astype(F32)
+            fb = f2_v[d].astype(BF)
             for acc in (im_hi, im_lo):
-                pltpu.matmul_acc_lhs(acc, fb[:, j * TILE:(j + 1) * TILE], j % 2)
-            if j + 2 < cuts:
-                push(j + 2)
+                pltpu.matmul_acc_lhs(acc, fb, d % 2)
+            if d + 2 < cuts:
+                push(d + 2)
         for n in range(min(2, Q // TILE)):
             push_q(n)
         im = pltpu.matmul_pop(im_hi) + pltpu.matmul_pop(im_lo)
@@ -238,29 +250,30 @@
         for n in range(Q // TILE):
             sc = pltpu.matmul_pop(outs[n])
             sc = sc[:E] + sc[E:2 * E]
-            for i in range(TILE // 128):
-                sc_v[n * (TILE // 128) + i] = sc[:, i * 128:(i + 1) * 128]
+            for i in range(TILE // span):
+                at = slice(i * span, (i + 1) * span)
+                sc_v[n * (TILE // span) + i] = jnp.concatenate(
+                    [sc[j:j + deep, at] for j in range(0, E, deep)], axis=1)
 
     tall = im2_v.shape[0]
     pl.run_scoped(
         score,
         *[pltpu.ACC(u)((tall, TILE), F32) for u in (0, 1)],
         *[pltpu.ACC(n % 2)((tall, TILE), F32) for n in range(Q // TILE)])
-    per = T // tiles
     me = t * H + h
 
     def ssend(d):
         pt = lax.rem(t + lax.rem(d, T), T)
         ph = lax.rem(h + lax.div(d, T), H)
         return pltpu.make_async_remote_copy(
-            sc_v.at[lax.div(pt, per)], s_v.at[me], ss_sem, sr_sem,
+            sc_v.at[pt], s_v.at[me], ss_sem, sr_sem,
             device_id=(pt, ph), device_id_type=MESH)
 
     def loop(fn):
         lax.fori_loop(1, T * H, lambda d, c: (fn(d), c)[1], 0, unroll=T * H <= 32)
 
     loop(lambda d: ssend(d).start())
-    s_v[me] = sc_v[lax.div(t, per)]
+    s_v[me] = sc_v[t]
     for cp in hid_out + hid_in:
         cp.wait_send()
     for n in range(half):
@@ -274,11 +287,7 @@
         tot = parts[0]
     else:
         tot = lax.fori_loop(0, T * H, lambda i, c: c + s_v[i], jnp.zeros(s_v.shape[1:], F32))
-    span = 128 // per
-    place = lax.rem(t, per)
-    res = tot[:, :span]
-    for i in range(1, per):
-        res = jnp.where(place == i, tot[:, i * span:(i + 1) * span], res)
+    res = jnp.concatenate([tot[:, i * span:(i + 1) * span] for i in range(E // deep)], axis=0)
     scores_out[...] = res
     pltpu.make_async_copy(got, got, ss_sem).wait()
     pltpu.make_async_copy(rs_r, rs_r, as_sem).wait()
@@ -304,8 +313,10 @@
     lanes = 2 * width
     cols = slab * width
     Q, M = queries.shape
-    ci, co = 14, 4
+    ci, co = 7, 2
     tall = -(-2 * E // 16) * 16
+    deep = E * (Q // T) // 128
+    cuts = half * lanes // TILE
     D = pltpu.SemaphoreType.DMA
     V = pltpu.VMEM
     hbm = pl.BlockSpec(memory_space=pltpu.HBM)
@@ -328,10 +339,10 @@
             V((E * slab, lanes), F32), V((E * slab, tokens), F32),
             V((half, E, lanes), F32), V((A - 1, part, E, lanes), F32),
             V((B, half, E, lanes), F32), V((half, E, lanes), F32),
-            V((tall, half * lanes), F32), V((tall, TILE), F32),
-            V((Q // 128, E, 128), F32), V((T * H, E, 128), F32),
+            V((cuts, tall, TILE), F32), V((tall, TILE), F32),
+            V((T, deep, 128), F32), V((T * H, deep, 128), F32),
             D((5 + co + 2 * ci,)), D, D((2, H - 1)), D((2, H - 1)),
-            D, D, D, D((B,)),
+            D, D, D, D((B, cuts)),
             D, D,
         ],
         compiler_params=pltpu.CompilerParams(

time: 24 us -> 23.7 us (0.987)
  Pallas kernels: 23.2 us -> 22.9 us
    pallas_call x1, Pallas kernels: 22.6 us -> 22.3 us  [on_device(): pl.pallas_call(functools.partial(kernel, T, H, A, E, ci, co), out_shape=(...]
where the time goes in v4:
time: 23.7 us; the launch traced here: 23.6 us
  Pallas kernels  22.9 us (97%)
  between operations  0.64 us (3%)
    pallas_call x1, Pallas kernels, on_device(): pl.pallas_call(functools.partial(kernel, T, H, A, E, ci, co), out_shape=(...  22.3 us
    pallas_call x1, Pallas kernels, on_device(): pl.pallas_call(finish, out_shape=(jax.ShapeDtypeStruct(scores.shape, F32)...  0.62 us

profile of v4, /device:TPU:0, one launch (start us, length us, event | category | flops | bytes accessed | tf_op | source)
XLA Modules:
  0.0 23.6 jit_solution(4129093568458587855)
XLA Ops:
  0.6 22.3 %shard_map.86 = (f32[4,64]{1,0:T(4,128)S(1)}, f32[4,2048]{1,0:T(4,128)S(1)}) custom-call(bf16[256,14336]{1,0:T(8,128)(2,1)} %acts.1, bf16[256,4096]{1,0:T(8,128)(2,1)} %grads.1, bf16[64,14336]{1,0:T(8,128)(2,1)} %bitcast.4, bf16[64,4096]{1,0:T(8,128)(2,1)} %bitcast.5, s32[1,256]{1,0:T(1,128)} %bitcast.6, f32[1024,256]{1,0:T(8,128)} %queries.1, ...), custom_call_target="tpu_custom_call" | custom-call | tf_op jit(solution)/shard_map/pallas_call | solution.py:323
  22.9 0.6 %shard_map.87 = (f32[4,64]{1,0:T(4,128)}, f32[4,2048]{1,0:T(4,128)}) custom-call(f32[4,64]{1,0:T(4,128)S(1)} %get-tuple-element.6.scores, f32[4,2048]{1,0:T(4,128)S(1)} %get-tuple-element.7.feats), custom_call_target="tpu_custom_call" | custom-call | tf_op jit(solution)/shard_map/pallas_call | solution.py:353

commit v5 on v4

--- a/solution.py
+++ b/solution.py
@@ -196,6 +196,28 @@
     Q = q_hi.shape[0]
     span = Q // T
     deep = E * span // 128
+    stripes, owners = Q // TILE, TILE // span
+    me = t * H + h
+
+    def stripe(n):
+        return lax.rem(lax.div(t, owners) + n + 1, stripes)
+
+    def ssend(base, d):
+        pt = base + lax.rem(lax.rem(t, owners) + lax.rem(d, owners), owners)
+        ph = lax.rem(h + lax.div(d, owners), H)
+        return pltpu.make_async_remote_copy(
+            sc_v.at[pt], s_v.at[me], ss_sem, sr_sem, device_id=(pt, ph), device_id_type=MESH)
+
+    def ship(n, sc):
+        base = stripe(n) * owners
+        sc = sc[:E] + sc[E:2 * E]
+        for i in range(owners):
+            at = slice(i * span, (i + 1) * span)
+            sc_v[base + i] = jnp.concatenate(
+                [sc[j:j + deep, at] for j in range(0, E, deep)], axis=1)
+        lax.fori_loop(
+            1 if n == stripes - 1 else 0, owners * H,
+            lambda d, c: (ssend(base, d).start(), c)[1], 0, unroll=T * H <= 32)
 
     def score(im_hi, im_lo, *outs):
         G = min(4, cuts)
@@ -212,7 +234,8 @@
 
         def push_q(n):
             for slot, q in enumerate((q_hi, q_lo)):
-                pltpu.matmul_push_rhs(q[pl.ds(n * TILE, TILE), :], slot, n % 2, transpose=True)
+                k = pl.ds(pl.multiple_of(stripe(n) * TILE, TILE), TILE)
+                pltpu.matmul_push_rhs(q[k, :], slot, n % 2, transpose=True)
 
         for n in range(min(2, len(rows))):
             push(n)
@@ -242,37 +265,20 @@
         im2_v[pl.ds(0, E), pl.ds(0, M)] = im
         im2_v[pl.ds(E, E), pl.ds(0, M)] = im - im.astype(BF).astype(F32)
         ib = im2_v[...].astype(BF)
-        for n in range(Q // TILE):
+        for n in range(stripes):
             for slot in range(2):
                 pltpu.matmul_acc_lhs(outs[n], ib, slot)
-            if n + 2 < Q // TILE:
+            if n + 2 < stripes:
                 push_q(n + 2)
-        for n in range(Q // TILE):
-            sc = pltpu.matmul_pop(outs[n])
-            sc = sc[:E] + sc[E:2 * E]
-            for i in range(TILE // span):
-                at = slice(i * span, (i + 1) * span)
-                sc_v[n * (TILE // span) + i] = jnp.concatenate(
-                    [sc[j:j + deep, at] for j in range(0, E, deep)], axis=1)
+            if n % 2 or n == stripes - 1:
+                for m in range(n - n % 2, n + 1):
+                    ship(m, pltpu.matmul_pop(outs[m]))
 
     tall = im2_v.shape[0]
     pl.run_scoped(
         score,
         *[pltpu.ACC(u)((tall, TILE), F32) for u in (0, 1)],
         *[pltpu.ACC(n % 2)((tall, TILE), F32) for n in range(Q // TILE)])
-    me = t * H + h
-
-    def ssend(d):
-        pt = lax.rem(t + lax.rem(d, T), T)
-        ph = lax.rem(h + lax.div(d, T), H)
-        return pltpu.make_async_remote_copy(
-            sc_v.at[pt], s_v.at[me], ss_sem, sr_sem,
-            device_id=(pt, ph), device_id_type=MESH)
-
-    def loop(fn):
-        lax.fori_loop(1, T * H, lambda d, c: (fn(d), c)[1], 0, unroll=T * H <= 32)
-
-    loop(lambda d: ssend(d).start())
     s_v[me] = sc_v[t]
     for cp in hid_out + hid_in:
         cp.wait_send()

time: 23.7 us -> 23.7 us (level)
  no operation moved by 1% of the time
where the time goes in v5:
time: 23.7 us; the launch traced here: 23.5 us
  Pallas kernels  22.9 us (97%)
  between operations  0.64 us (3%)
    pallas_call x1, Pallas kernels, on_device(): pl.pallas_call(functools.partial(kernel, T, H, A, E, ci, co), out_shape=(...  22.3 us
    pallas_call x1, Pallas kernels, on_device(): pl.pallas_call(finish, out_shape=(jax.ShapeDtypeStruct(scores.shape, F32)...  0.62 us

profile of v5, /device:TPU:0, one launch (start us, length us, event | category | flops | bytes accessed | tf_op | source)
XLA Modules:
  0.0 23.5 jit_solution(1797049983722337615)
XLA Ops:
  0.6 22.3 %shard_map.86 = (f32[4,64]{1,0:T(4,128)S(1)}, f32[4,2048]{1,0:T(4,128)S(1)}) custom-call(bf16[256,14336]{1,0:T(8,128)(2,1)} %acts.1, bf16[256,4096]{1,0:T(8,128)(2,1)} %grads.1, bf16[64,14336]{1,0:T(8,128)(2,1)} %bitcast.4, bf16[64,4096]{1,0:T(8,128)(2,1)} %bitcast.5, s32[1,256]{1,0:T(1,128)} %bitcast.6, f32[1024,256]{1,0:T(8,128)} %queries.1, ...), custom_call_target="tpu_custom_call" | custom-call | tf_op jit(solution)/shard_map/pallas_call | solution.py:329
  22.9 0.6 %shard_map.87 = (f32[4,64]{1,0:T(4,128)}, f32[4,2048]{1,0:T(4,128)}) custom-call(f32[4,64]{1,0:T(4,128)S(1)} %get-tuple-element.6.scores, f32[4,2048]{1,0:T(4,128)S(1)} %get-tuple-element.7.feats), custom_call_target="tpu_custom_call" | custom-call | tf_op jit(solution)/shard_map/pallas_call | solution.py:359
